TPU v7x, 256 devices: a whole 4x4x8 slice. The times are simulated.
256 devices in a mesh: ctx: 32 (over y, z_lo, core), ch: 8 (over z_hi, x).
Axes of the slice: x: 4, y: 4, z: 8 (z_hi: 2, z_lo: 4; z = z_hi * 4 + z_lo), core: 2. Of those that a mesh axis runs over, the one named last changes fastest.
Arguments:
- token_ids: int32 [16384], P('ctx'), may hold values from 65 to 84, as said below
- embedding: bfloat16 [512, 4096], P(None, 'ch'), may hold values from -6 to 6
- long_table: bfloat16 [512, 3, 4096], P(None, None, 'ch'), may hold values from -6 to 6
- long_taps: float32 [3, 3, 4096], P(None, None, 'ch'), may hold values from -3 to 3
- long_residue: float32 [256, 16], P('ch'), may hold values from -1.5 to 1.5
- long_rate: float32 [256, 16], P('ch'), may hold values from 1.2207031e-06 to 0.04
- long_skip: float32 [4096], P('ch'), may hold values from 0.25 to 1.75
- medium_gain: bfloat16 [4096], P('ch'), may hold values from 0.25 to 1.75
- medium_weight: bfloat16 [4096, 3, 4096], P('ctx', None, 'ch'), may hold values from -0.09375 to 0.09375
- medium_taps: float32 [3, 3, 4096], P(None, None, 'ch'), may hold values from -3 to 3
- medium_group_filter: float32 [256, 128], P('ch'), may hold values from -0.6 to 0.6
- medium_skip: float32 [4096], P('ch'), may hold values from 0.25 to 1.75
- filter_group: int32 [4096], P('ch'), may hold values from 0 to 255, as said below
Outputs:
- block_output: bfloat16 [16384, 4096], P('ctx', 'ch')
Inputs may be any that keep to these rules, and one draw needn't show every extreme that they name: `token_ids`: every token is the byte code of A, C, G, T or N. `filter_group`: each filter group has exactly 16 channels, all within one block of 512 consecutive channels; block j holds groups j * (32) to (j + 1) * 32 - 1.
All inputs are finite; a program needn't handle non-finite values.
Results may differ from a plain program's by a relative error of at most 0.006.
Values may be sent and summed in bfloat16 or wider, within the bound.
A program may use at most 128 MiB of HBM per device.

v0:
```python
import jax
import jax.numpy as jnp
from jax import lax
from jax.sharding import PartitionSpec as P

MODEL_WIDTH = 4096
epsilon = 1e-06


def from_behind(x, axis, by):
    count = lax.axis_size(axis)
    pairs = [(i, i + by) for i in range(count) if 0 <= i + by < count]
    return lax.ppermute(x, axis, pairs)


def carried_in(value, axis, join, neutral):
    count, mine = (lax.axis_size(axis), lax.axis_index(axis))
    pieces = jax.tree.map(lambda part: lax.all_gather(part, axis), value)
    running = jax.tree.map(
        lambda part, zero: jnp.full_like(part, 0) + jnp.asarray(zero, part.dtype), value, neutral
    )

    def turn(position, running):
        longer = join(running, jax.tree.map(lambda part: part[position], pieces))
        return jax.tree.map(lambda new, old: jnp.where(position < mine, new, old), longer, running)

    return lax.fori_loop(0, count - 1, turn, running)


def featurize(streams, before, filter_taps):
    extended = jnp.concatenate([before, streams], axis=0).astype(jnp.float32)
    length = streams.shape[0]
    mixed = filter_taps[0] * extended[2 : 2 + length]
    mixed = mixed + filter_taps[1] * extended[1 : 1 + length]
    mixed = mixed + filter_taps[2] * extended[0:length]
    return mixed


def previous_rows(values, count):
    return from_behind(values[values.shape[0] - count :], "ctx", 1)


def chain_combine(earlier, later):
    return (earlier[0] * later[0], earlier[1] * later[0] + later[1])


def split_product(form, data, table):
    upper = table.astype(jnp.bfloat16)
    lower = (table - upper.astype(jnp.float32)).astype(jnp.bfloat16)
    first = jnp.einsum(form, data, upper, preferred_element_type=jnp.float32)
    return first + jnp.einsum(form, data, lower, preferred_element_type=jnp.float32)


def local(
    token_ids,
    embedding,
    long_table,
    long_taps,
    long_residue,
    long_rate,
    long_skip,
    medium_gain,
    medium_weight,
    medium_taps,
    medium_group_filter,
    medium_skip,
    filter_group,
):
    tokens = token_ids.shape[0]
    channels = embedding.shape[1]
    vocab = embedding.shape[0]
    groups = long_rate.shape[0]
    pole_count = long_rate.shape[1]
    tap_count = medium_group_filter.shape[1]
    members = channels // groups
    blocks = tokens // tap_count
    one_hot = (token_ids[:, None] == jnp.arange(vocab, dtype=jnp.int32)[None, :]).astype(
        jnp.bfloat16
    )
    resid = jnp.dot(one_hot, embedding, preferred_element_type=jnp.float32)
    streams = jnp.dot(
        one_hot, long_table.reshape(vocab, 3 * channels), preferred_element_type=jnp.float32
    )
    streams = streams.astype(jnp.bfloat16).reshape(tokens, 3, channels)
    local_group = filter_group - lax.axis_index("ch") * groups
    channel_ids = jnp.arange(channels, dtype=jnp.int32)
    same_group = local_group[:, None] == local_group[None, :]
    rank_within = jnp.sum(same_group & (channel_ids[None, :] < channel_ids[:, None]), axis=1)
    placed = local_group * members + rank_within
    select = placed[:, None] == channel_ids[None, :]
    select_half = select.astype(jnp.bfloat16)
    select_wide = select.astype(jnp.float32)

    def grouped(values):
        length = values.shape[0]
        moved = jnp.dot(values, select_half, preferred_element_type=jnp.float32).astype(
            jnp.bfloat16
        )
        return moved.reshape(length, groups, members).transpose(1, 2, 0)

    def ungrouped(values):
        length = values.shape[-1]
        flat = values.transpose(2, 0, 1).reshape(length, channels)
        return jnp.dot(
            flat, select_wide.T, precision=lax.Precision.HIGHEST, preferred_element_type=jnp.float32
        )

    before = previous_rows(streams, 2)
    mixed = featurize(streams, before, long_taps)
    query = mixed[:, 0]
    product = (mixed[:, 1] * mixed[:, 2]).astype(jnp.bfloat16)
    product_wide = product.astype(jnp.float32)
    positions = jnp.arange(tap_count, dtype=jnp.float32)
    weight_res = long_residue * jnp.sqrt(-jnp.expm1(-2.0 * long_rate))
    kernel = jnp.sum(weight_res[:, :, None] * jnp.exp(-long_rate[:, :, None] * positions), axis=1)
    offsets = jnp.arange(tap_count, dtype=jnp.int32)
    lag = offsets[None, :] - offsets[:, None]
    toeplitz = jnp.where(lag[None] >= 0, kernel[:, jnp.clip(lag, 0, tap_count - 1)], 0.0)
    blocked = grouped(product).reshape(groups, members, blocks, tap_count)
    inner = split_product("gcns,gst->gcnt", blocked, toeplitz)
    ending = jnp.exp(-long_rate[:, :, None] * (tap_count - 1.0 - positions))
    closing = split_product("gcns,gps->gcnp", blocked, ending)
    across = jnp.exp(-long_rate * tap_count)[:, None, :]
    summary = jnp.zeros((groups, members, pole_count), jnp.float32)
    for block in range(blocks):
        summary = summary * across + closing[:, :, block]
    whole_decay = jnp.broadcast_to(
        jnp.exp(-long_rate * tokens)[:, None, :], (groups, members, pole_count)
    )
    decay_flat = whole_decay.transpose(2, 0, 1).reshape(pole_count, channels)
    summary_flat = summary.transpose(2, 0, 1).reshape(pole_count, channels)
    identity = (
        jnp.ones((pole_count, channels), jnp.float32),
        jnp.zeros((pole_count, channels), jnp.float32),
    )
    carried = carried_in((decay_flat, summary_flat), "ctx", chain_combine, identity)[1]
    state = carried.reshape(pole_count, groups, members).transpose(1, 2, 0)
    starts = []
    for block in range(blocks):
        starts.append(state)
        state = state * across + closing[:, :, block]
    start_stack = jnp.stack(starts, axis=2)
    entry = weight_res[:, :, None] * jnp.exp(-long_rate[:, :, None] * (positions + 1.0))
    outer = jnp.einsum("gcnp,gpt->gcnt", start_stack, entry, precision=lax.Precision.HIGHEST)
    conv_long = (
        ungrouped((inner + outer).reshape(groups, members, tokens)) + long_skip * product_wide
    )
    middle = (resid + query * conv_long).astype(jnp.bfloat16)
    middle_wide = middle.astype(jnp.float32)
    squares = lax.psum(jnp.sum(middle_wide * middle_wide, axis=1), "ch")
    scale = lax.rsqrt(squares / MODEL_WIDTH + epsilon)
    normed = (middle_wide * scale[:, None] * medium_gain.astype(jnp.float32)).astype(jnp.bfloat16)
    features = lax.all_gather(normed, "ch", axis=1, tiled=True)
    piece = lax.all_gather(medium_weight, "ctx", axis=0, tiled=True)
    projected = jnp.dot(
        features, piece.reshape(piece.shape[0], 3 * channels), preferred_element_type=jnp.float32
    )
    projected = projected.astype(jnp.bfloat16).reshape(tokens, 3, channels)
    before2 = previous_rows(projected, 2)
    mixed2 = featurize(projected, before2, medium_taps)
    product2 = (mixed2[:, 1] * mixed2[:, 2]).astype(jnp.bfloat16)
    margin = previous_rows(product2, tap_count)
    query2 = mixed2[:, 0]
    second_product_wide = product2.astype(jnp.float32)
    extended = jnp.concatenate([margin, product2], axis=0)
    framed = grouped(extended).reshape(groups, members, blocks + 1, tap_count)
    windows = jnp.concatenate([framed[:, :, :-1], framed[:, :, 1:]], axis=-1)
    wide_offsets = jnp.arange(2 * tap_count, dtype=jnp.int32)
    tap_delay = offsets[None, :] + tap_count - wide_offsets[:, None]
    valid = (tap_delay >= 0) & (tap_delay < tap_count)
    banded = jnp.where(
        valid[None], medium_group_filter[:, jnp.clip(tap_delay, 0, tap_count - 1)], 0.0
    )
    medium = split_product("gcns,gst->gcnt", windows, banded)
    medium_convolution = (
        ungrouped(medium.reshape(groups, members, tokens)) + medium_skip * second_product_wide
    )
    return (middle_wide + query2 * medium_convolution).astype(jnp.bfloat16)


def solution(mesh):
    in_specs = (
        P("ctx"),
        P(None, "ch"),
        P(None, None, "ch"),
        P(None, None, "ch"),
        P("ch", None),
        P("ch", None),
        P("ch"),
        P("ch"),
        P("ctx", None, "ch"),
        P(None, None, "ch"),
        P("ch", None),
        P("ch"),
        P("ch"),
    )
    out_specs = P("ctx", "ch")
    return jax.shard_map(local, mesh=mesh, in_specs=in_specs, out_specs=out_specs, check_vma=False)
```

profile of v0, /device:TPU:8, one launch (start us, length us, event | category | flops | bytes accessed | tf_op | source)
XLA Modules:
  0.0 565.7 jit_solution(1877062003630645721)
XLA Ops:
  6.5 1.8 copy.92
  8.4 1.0 convolution_convert_fusion.1
  9.4 1.2 copy-done.10
  10.9 1.9 collective-permute-start
  14.1 1.7 copy.94
  16.1 6.6 %collective-permute-done = bf16[2,3,512]{0,2,1:T(8,128)(2,1)S(1)} collective-permute-done((bf16[2,3,512]{0,2,1:T(8,128)(2,1)S(1)}, bf16[2,3,512]{0,2,1:T(8,128)(2,1)S(1)}, u32[]{:S(2)}, u32[]{:S(2)}) %collective-permute-start) | collective-permute-done | bytes 6176 | tf_op jit(solution)/shard_map/ppermute | solution.py:13
  22.7 0.9 maximum_convert_fusion
  23.5 2.8 fusion.4
  28.3 0.9 copy-done.5
  30.4 54.5 %gather_fusion = f32[16384,32]{1,0:T(8,128)} fusion(f32[32,128]{0,1:T(8,128)S(1)} %copy.97, s32[16384]{0:T(1024)S(1)} %fusion.91), kind=kCustom, calls=%fused_computation | custom fusion | bytes 4259840 | tf_op jit(solution)/shard_map/gather | solution.py:118
  84.9 5.6 copy.98
  90.6 1.6 fusion.44
  92.2 1.4 fusion.26
  93.6 42.2 %all-gather.7.cloned.1.call-done = f32[32,16,512]{2,1,0:T(8,128)} async-done(((f32[1,16,512]{2,1,0:T(8,128)}), f32[32,16,512]{2,1,0:T(8,128)}) %all-gather.7.cloned.1.call-update) | async-done | bytes 1048592 | tf_op jit(solution)/shard_map/all_gather | solution.py:18
  135.7 25.2 %while.14 = (s32[]{:T(128)}, f32[16,512]{1,0:T(8,128)S(1)}, s32[]{:T(128)}, f32[32,16,512]{2,1,0:T(8,128)}, f32[32,16,512]{2,1,0:T(8,128)}, /*index=5*/s32[]{:T(128)}, s32[]{:T(128)}) while((s32[]{:T(128)}, f32[16,512]{1,0:T(8,128)S(1)}, s32[]{:T(128)}, f32[32,16,512]{2,1,0:T(8,128)}, f32[32,16,512]{2,1,0:T(8,128)}, ...), condition=%wide.region_3.4_spmd.clone, body=%wide.region_2.3_spmd.clone.sunk | while | flops 32772 | bytes 131173 | solution.py:27
  136.5 0.8 fusion.110
  137.4 0.8 fusion.110
  138.2 0.8 fusion.110
  139.0 0.8 fusion.110
  139.8 0.8 fusion.110
  140.6 0.8 fusion.110
  141.4 0.8 fusion.110
  142.2 0.8 fusion.110
  143.0 0.8 fusion.110
  143.9 0.8 fusion.110
  144.7 0.8 fusion.110
  145.5 0.8 fusion.110
  146.3 0.8 fusion.110
  147.1 0.8 fusion.110
  147.9 0.8 fusion.110
  148.7 0.8 fusion.110
  149.5 0.8 fusion.110
  150.4 0.8 fusion.110
  151.2 0.8 fusion.110
  152.0 0.8 fusion.110
  152.8 0.8 fusion.110
  153.6 0.8 fusion.110
  154.4 0.8 fusion.110
  155.2 0.8 fusion.110
  156.0 0.8 fusion.110
  156.9 0.8 fusion.110
  157.7 0.8 fusion.110
  158.5 0.8 fusion.110
  161.0 1.3 fusion.89
  162.3 1.1 fusion.40
  164.8 2.6 fusion.28
  167.4 29.8 %psum.7 = f32[512]{0:T(512)S(1)} all-reduce(f32[512]{0:T(512)S(1)} %get-tuple-element.144), channel_id=1, replica_groups=mesh['ctx'=32,'ch'=8] {'ch'}, use_global_device_ids=true, to_apply=%region_5.6 | all-reduce | flops 512 | bytes 4096 | tf_op jit(solution)/shard_map/psum | solution.py:150
  197.2 0.9 fusion.30
  198.4 0.9 copy.112
  199.5 100.5 %all-gather.9.cloned.1.call-done = bf16[512,4096]{0,1:T(8,128)(2,1)} async-done(((bf16[512,512]{0,1:T(8,128)(2,1)}), bf16[512,4096]{0,1:T(8,128)(2,1)}) %all-gather.9.cloned.1.call-update) | async-done | bytes 4194320 | tf_op jit(solution)/shard_map/all_gather | solution.py:153
  300.0 101.1 %all-gather.11.cloned.1.call-done = bf16[4096,3,512]{0,2,1:T(8,128)(2,1)} async-done(((bf16[128,3,512]{0,2,1:T(8,128)(2,1)}), bf16[4096,3,512]{0,2,1:T(8,128)(2,1)}) %all-gather.11.cloned.1.call-update) | async-done | bytes 12582928 | tf_op jit(solution)/shard_map/all_gather | solution.py:154
  401.1 11.0 %convolution_convert_fusion = bf16[512,1536]{1,0:T(8,128)(2,1)S(1)} fusion(bf16[512,4096]{0,1:T(8,128)(2,1)} %all-gather.9.cloned.1.call-done, bf16[4096,1536]{0,1:T(8,128)(2,1)} %bitcast.244), kind=kOutput, calls=%fused_computation.18 | convolution fusion | flops 6443237376 | bytes 18350080 | tf_op jit(solution)/shard_map/dot_general | solution.py:155
  412.1 1.2 copy-done.11
  413.5 2.2 collective-permute-start.1
  415.8 108.5 %gather_fusion.1 = f32[32768,32]{1,0:T(8,128)} fusion(f32[32,128]{0,1:T(8,128)S(1)} %copy.117, s32[32768]{0:T(1024)S(1)} %fusion.78), kind=kCustom, calls=%fused_computation.1 | custom fusion | bytes 8519680 | tf_op jit(solution)/shard_map/gather | solution.py:172
  524.3 11.8 %copy.118 = f32[256,128,32]{1,0,2:T(8,128)} copy(f32[256,128,32]{2,1,0:T(8,128)} %bitcast.227) | data formatting | bytes 8388608 | tf_op jit(solution)/shard_map/gather | solution.py:172
  536.1 1.7 copy.114
  537.8 0.9 maximum_convert_fusion.1
  538.7 2.8 fusion.2
  541.6 3.4 collective-permute-start.2
  545.2 5.5 collective-permute-done.2
  552.8 1.5 copy-done.2
  555.7 2.4 fusion.31
  558.1 1.0 copy.121
  (104 shorter events, 13.3 us)
Async XLA Ops:
  6.5 84.0 %copy-start = (bf16[512,512]{1,0:T(8,128)(2,1)S(1)}, bf16[512,512]{1,0:T(8,128)(2,1)}, u32[]{:S(2)}) copy-start(bf16[512,512]{1,0:T(8,128)(2,1)} %param.16) | copy-start | bytes 1572868
  6.5 1.8 copy-start.19
  6.5 87.0 %all-gather.5.cloned.1.call-start = ((), (), s32[]{:S(2)}) async-start(), calls=%async_computation | async-start | bytes 1081344 | tf_op jit(solution)/shard_map/all_gather | solution.py:18
  8.3 4.5 copy-start.16
  8.3 4.5 copy-start.17
  8.4 5.5 copy-start.13
  8.4 5.5 copy-start.18
  9.4 1.2 copy-start.10
  10.9 11.8 %collective-permute-start = (bf16[2,3,512]{0,2,1:T(8,128)(2,1)S(1)}, bf16[2,3,512]{0,2,1:T(8,128)(2,1)S(1)}, u32[]{:S(2)}, u32[]{:S(2)}) collective-permute-start(bf16[2,3,512]{0,2,1:T(8,128)(2,1)S(1)} %bitcast.242), channel_id=1, source_target_pairs={{0,8},{8,16},{16,24},{24,32},{32,40},{40,48},{48,56},{56,64},{64,7... | collective-permute-start | bytes 18440 | tf_op jit(solution)/shard_map/ppermute | solution.py:13
  13.8 122.0 %all-gather.7.cloned.1.call-start = ((), (), s32[]{:S(2)}) async-start(), calls=%async_computation.1 | async-start | bytes 1081344 | tf_op jit(solution)/shard_map/all_gather | solution.py:18
  26.3 1.9 copy-start.4
  26.5 1.0 copy-start.8
  28.2 1.0 copy-start.5
  29.9 270.1 %all-gather.9.cloned.1.call-start = ((), (), s32[]{:S(2)}) async-start(), calls=%async_computation.2 | async-start | bytes 4718592 | tf_op jit(solution)/shard_map/all_gather | solution.py:153
  84.9 5.6 copy-start.22
  161.0 2.4 copy-start.7
  163.5 1.2 copy-start.6
  163.5 1.3 copy-start.9
  163.5 1.3 copy-start.20
  164.1 34.3 %copy-start.12 = (bf16[128,3,512]{2,0,1:T(8,128)(2,1)S(1)}, bf16[128,3,512]{2,0,1:T(8,128)(2,1)}, u32[]{:S(2)}) copy-start(bf16[128,3,512]{2,0,1:T(8,128)(2,1)} %param.23) | copy-start | bytes 1179652
  198.2 202.9 %all-gather.11.cloned.1.call-start = ((), (), s32[]{:S(2)}) async-start(), calls=%async_computation.3 | async-start | bytes 12976128 | tf_op jit(solution)/shard_map/all_gather | solution.py:154
  401.1 14.6 %copy-start.14 = (f32[3,3,512]{2,1,0:T(4,128)S(1)}, f32[3,3,512]{2,1,0:T(4,128)}, u32[]{:S(2)}) copy-start(f32[3,3,512]{2,1,0:T(4,128)} %param.24) | copy-start | bytes 55300
  401.1 14.6 %copy-start.15 = (f32[32,128]{1,0:T(8,128)S(1)}, f32[32,128]{1,0:T(8,128)}, u32[]{:S(2)}) copy-start(f32[32,128]{1,0:T(8,128)} %param.25) | copy-start | bytes 49156
  412.1 1.2 copy-start.11
  413.5 124.3 %collective-permute-start.1 = (bf16[2,3,512]{0,2,1:T(8,128)(2,1)S(1)}, bf16[2,3,512]{0,2,1:T(8,128)(2,1)S(1)}, u32[]{:S(2)}, u32[]{:S(2)}) collective-permute-start(bf16[2,3,512]{0,2,1:T(8,128)(2,1)S(1)} %bitcast.243), channel_id=1, source_target_pairs={{0,8},{8,16},{16,24},{24,32},{32,40},{40,48},{48,56},{56,64},{64,7... | collective-permute-start | bytes 18440 | tf_op jit(solution)/shard_map/ppermute | solution.py:13
  541.4 9.9 %copy-start.3 = (f32[512,3,512]{0,2,1:T(8,128)}, f32[512,3,512]{0,2,1:T(8,128)S(1)}, u32[]{:S(2)}) copy-start(f32[512,3,512]{0,2,1:T(8,128)S(1)} %fusion.2) | copy-start | bytes 9437188
  541.6 9.0 %collective-permute-start.2 = (bf16[128,512]{0,1:T(8,128)(2,1)S(1)}, bf16[128,512]{0,1:T(8,128)(2,1)S(1)}, u32[]{:S(2)}, u32[]{:S(2)}) collective-permute-start(bf16[128,512]{0,1:T(8,128)(2,1)S(1)} %slice_bitcast_fusion.6), channel_id=1, source_target_pairs={{0,8},{8,16},{16,24},{24,32},{32,40},{40,48},{48,56},{56,64},{64,7... | collective-permute-start | bytes 393224 | tf_op jit(solution)/shard_map/ppermute | solution.py:13
  552.1 2.2 copy-start.2
  554.7 0.9 copy-start.21
  554.8 4.4 copy-start.1
Sparse Core Ops, SparseCore 0:
  13.9 62.3 all-gather.4
  78.1 57.5 all-gather.6
  198.3 101.6 all-gather.8
  301.6 99.4 all-gather.10
where the time goes:
time: 568 us; the launch traced here: 566 us
  waiting for transfers between devices  256 us (45%)
  local copies, waits for them, and re-layouts  198 us (35%)
  other arithmetic  35.1 us (6%)
  blocking collectives  29.8 us (5%)
  matrix products  24.8 us (4%)
  between operations  13.8 us (2%)
  starting transfers between devices  7.75 us (1%)
    gather x2, local copies, waits for them, and re-layouts, local(): medium_group_filter[:, jnp.clip(tap_delay, 0, tap_count - 1)]  120 us
    all_gather x1, waiting for transfers between devices, local(): piece = lax.all_gather(medium_weight, 'ctx', axis=0, tiled=True)  101 us
    all_gather x1, waiting for transfers between devices, local(): features = lax.all_gather(normed, 'ch', axis=1, tiled=True)  101 us
    gather x2, local copies, waits for them, and re-layouts, local(): kernel[:, jnp.clip(lag, 0, tap_count - 1)]  60 us
    all_gather x2, waiting for transfers between devices, carried_in(): pieces = jax.tree.map(lambda part: lax.all_gather(part, axis), value)  42.2 us
    psum x1, blocking collectives, local(): squares = lax.psum(jnp.sum(middle_wide * middle_wide, axis=1), 'ch')  29.8 us
    select_n x31, other arithmetic, turn(): jnp.where(position < mine, new, old)  24.4 us
    ppermute x3, waiting for transfers between devices, from_behind(): return lax.ppermute(x, axis, pairs)  12 us
  transfers between devices with their start and end apart: 7, of which 5 were waited for; matrix products, arithmetic and copies ran while one was open for 35% of the time, Pallas kernels for 0%

commit v1 on v0

--- a/solution.py
+++ b/solution.py
@@ -151,7 +151,9 @@
     scale = lax.rsqrt(squares / MODEL_WIDTH + epsilon)
     normed = (middle_wide * scale[:, None] * medium_gain.astype(jnp.float32)).astype(jnp.bfloat16)
     features = lax.all_gather(normed, "ch", axis=1, tiled=True)
-    piece = lax.all_gather(medium_weight, "ctx", axis=0, tiled=True)
+    piece = jnp.concatenate(
+        lax.all_to_all(jnp.stack([medium_weight] * lax.axis_size("ctx")), "ctx", 0, 0), axis=0
+    )
     projected = jnp.dot(
         features, piece.reshape(piece.shape[0], 3 * channels), preferred_element_type=jnp.float32
     )

time: 568 us -> 710 us (1.25)
  waiting for transfers between devices: 256 us -> 364 us
  local copies, waits for them, and re-layouts: 198 us -> 221 us
  starting transfers between devices: 7.75 us -> 16.4 us
    ppermute x3, waiting for transfers between devices: 12 us -> 211 us  [from_behind(): return lax.ppermute(x, axis, pairs)]
    all_gather x1 -> x0, waiting for transfers between devices: 101 us -> none  [local(): piece = lax.all_gather(medium_weight, 'ctx', axis=0, tiled=True)]
    all_gather x2, waiting for transfers between devices: 42.2 us -> 58.1 us  [carried_in(): pieces = jax.tree.map(lambda part: lax.all_gather(part, axis), value)]
    all_to_all x0 -> x1, local copies, waits for them, and re-layouts: none -> 14.5 us  [local(): lax.all_to_all(jnp.stack([medium_weight] * lax.axis_size('ctx')), 'ctx',...]
    all_to_all x0 -> x1, starting transfers between devices: none -> 9.32 us  [local(): lax.all_to_all(jnp.stack([medium_weight] * lax.axis_size('ctx')), 'ctx',...]
    another operation x0 -> x1, local copies, waits for them, and re-layouts: none -> 7.62 us  [local(): jnp.stack([medium_weight] * lax.axis_size('ctx'))]
  transfers between devices with their start and end apart: 7 -> 7, of which waited for: 5 -> 4; matrix products, arithmetic and copies ran while one was open for 35% -> 35% of each run, Pallas kernels for 0% -> 0%
where the time goes in v1:
time: 710 us; the launch traced here: 707 us
  waiting for transfers between devices  364 us (51%)
  local copies, waits for them, and re-layouts  221 us (31%)
  other arithmetic  35.1 us (5%)
  blocking collectives  29.8 us (4%)
  matrix products  26.9 us (4%)
  starting transfers between devices  16.4 us (2%)
  between operations  13.8 us (2%)
    ppermute x3, waiting for transfers between devices, from_behind(): return lax.ppermute(x, axis, pairs)  211 us
    gather x2, local copies, waits for them, and re-layouts, local(): medium_group_filter[:, jnp.clip(tap_delay, 0, tap_count - 1)]  121 us
    all_gather x1, waiting for transfers between devices, local(): features = lax.all_gather(normed, 'ch', axis=1, tiled=True)  94.2 us
    gather x2, local copies, waits for them, and re-layouts, local(): kernel[:, jnp.clip(lag, 0, tap_count - 1)]  60.3 us
    all_gather x2, waiting for transfers between devices, carried_in(): pieces = jax.tree.map(lambda part: lax.all_gather(part, axis), value)  58.1 us
    psum x1, blocking collectives, local(): squares = lax.psum(jnp.sum(middle_wide * middle_wide, axis=1), 'ch')  29.8 us
    select_n x31, other arithmetic, turn(): jnp.where(position < mine, new, old)  24.4 us
    all_to_all x1, local copies, waits for them, and re-layouts, local(): lax.all_to_all(jnp.stack([medium_weight] * lax.axis_size('ctx')), 'ctx',...  14.5 us
  transfers between devices with their start and end apart: 7, of which 4 were waited for; matrix products, arithmetic and copies ran while one was open for 35% of the time, Pallas kernels for 0%

profile of v1, /device:TPU:8, one launch (start us, length us, event | category | flops | bytes accessed | tf_op | source)
XLA Modules:
  0.0 707.4 jit_solution(4822329252907276250)
XLA Ops:
  6.5 1.3 copy.114
  7.8 7.6 %stack.17 = bf16[32,128,3,512]{1,3,2,0:T(8,128)(2,1)} broadcast(bf16[128,3,512]{0,2,1:T(8,128)(2,1)S(1)} %copy.114), dimensions={1,2,3} | broadcast | bytes 12976128 | tf_op jit(solution)/shard_map/stack | solution.py:155
  15.4 9.3 %all-to-all-start = ((bf16[32,128,3,512]{1,3,2,0:T(8,128)(2,1)}), bf16[32,128,3,512]{1,3,2,0:T(8,128)(2,1)}, u32[]{:S(2)}, u32[]{:S(2)}) async-start(bf16[32,128,3,512]{1,3,2,0:T(8,128)(2,1)} %stack.17), calls=%async_computation | async-start | bytes 25165824 | tf_op jit(solution)/shard_map/all_to_all | solution.py:155
  24.8 1.6 copy.94
  26.5 2.5 convolution_convert_fusion
  28.9 1.2 copy-done.10
  30.4 2.0 collective-permute-start
  33.8 1.7 copy.96
  35.7 205.2 %collective-permute-done = bf16[2,3,512]{0,2,1:T(8,128)(2,1)S(1)} collective-permute-done((bf16[2,3,512]{0,2,1:T(8,128)(2,1)S(1)}, bf16[2,3,512]{0,2,1:T(8,128)(2,1)S(1)}, u32[]{:S(2)}, u32[]{:S(2)}) %collective-permute-start) | collective-permute-done | bytes 6176 | tf_op jit(solution)/shard_map/ppermute | solution.py:13
  240.9 0.9 maximum_convert_fusion
  241.8 2.8 fusion.7
  246.5 0.9 copy-done.5
  248.8 54.8 %gather_fusion = f32[16384,32]{1,0:T(8,128)} fusion(f32[32,128]{0,1:T(8,128)S(1)} %copy.99, s32[16384]{0:T(1024)S(1)} %fusion.97), kind=kCustom, calls=%fused_computation | custom fusion | bytes 4259840 | tf_op jit(solution)/shard_map/gather | solution.py:118
  303.6 5.5 copy.100
  309.2 1.7 fusion.50
  310.9 1.4 fusion.32
  312.3 58.1 %all-gather.6.cloned.1.call-done = f32[32,16,512]{2,1,0:T(8,128)} async-done(((f32[1,16,512]{2,1,0:T(8,128)}), f32[32,16,512]{2,1,0:T(8,128)}) %all-gather.6.cloned.1.call-update) | async-done | bytes 1048592 | tf_op jit(solution)/shard_map/all_gather | solution.py:18
  370.4 25.2 %while.14 = (s32[]{:T(128)}, f32[16,512]{1,0:T(8,128)S(1)}, s32[]{:T(128)}, f32[32,16,512]{2,1,0:T(8,128)}, f32[32,16,512]{2,1,0:T(8,128)}, /*index=5*/s32[]{:T(128)}, s32[]{:T(128)}) while((s32[]{:T(128)}, f32[16,512]{1,0:T(8,128)S(1)}, s32[]{:T(128)}, f32[32,16,512]{2,1,0:T(8,128)}, f32[32,16,512]{2,1,0:T(8,128)}, ...), condition=%wide.region_3.4_spmd.clone, body=%wide.region_2.3_spmd.clone.sunk | while | flops 32772 | bytes 131173 | solution.py:27
  371.3 0.8 fusion.115
  372.1 0.8 fusion.115
  372.9 0.8 fusion.115
  373.7 0.8 fusion.115
  374.5 0.8 fusion.115
  375.3 0.8 fusion.115
  376.1 0.8 fusion.115
  376.9 0.8 fusion.115
  377.8 0.8 fusion.115
  378.6 0.8 fusion.115
  379.4 0.8 fusion.115
  380.2 0.8 fusion.115
  381.0 0.8 fusion.115
  381.8 0.8 fusion.115
  382.6 0.8 fusion.115
  383.4 0.8 fusion.115
  384.2 0.8 fusion.115
  385.1 0.8 fusion.115
  385.9 0.8 fusion.115
  386.7 0.8 fusion.115
  387.5 0.8 fusion.115
  388.3 0.8 fusion.115
  389.1 0.8 fusion.115
  389.9 0.8 fusion.115
  390.7 0.8 fusion.115
  391.6 0.8 fusion.115
  395.7 1.3 fusion.95
  397.0 1.1 fusion.46
  399.5 2.6 fusion.34
  402.1 29.8 %psum.7 = f32[512]{0:T(512)S(1)} all-reduce(f32[512]{0:T(512)S(1)} %get-tuple-element.144), channel_id=1, replica_groups=mesh['ctx'=32,'ch'=8] {'ch'}, use_global_device_ids=true, to_apply=%region_5.6 | all-reduce | flops 512 | bytes 4096 | tf_op jit(solution)/shard_map/psum | solution.py:150
  431.9 0.9 fusion.36
  433.0 14.5 %copy.115 = bf16[32,128,3,512]{1,0,3,2:T(8,128)(2,1)} copy(bf16[32,128,3,512]{1,3,2,0:T(8,128)(2,1)} %all-to-all-done) | data formatting | bytes 25165824 | tf_op jit(solution)/shard_map/all_to_all | solution.py:155
  447.6 94.2 %all-gather.8.cloned.1.call-done = bf16[512,4096]{0,1:T(8,128)(2,1)} async-done(((bf16[512,512]{0,1:T(8,128)(2,1)}), bf16[512,4096]{0,1:T(8,128)(2,1)}) %all-gather.8.cloned.1.call-update) | async-done | bytes 4194320 | tf_op jit(solution)/shard_map/all_gather | solution.py:153
  541.8 11.5 %fusion.9 = bf16[512,1536]{1,0:T(8,128)(2,1)S(1)} fusion(bf16[512,4096]{0,1:T(8,128)(2,1)} %all-gather.8.cloned.1.call-done, bf16[192,8,32,128]{3,2,1,0:T(8,128)(2,1)} %bitcast.236), kind=kOutput, calls=%fused_computation.21 | convolution fusion | flops 6443237376 | bytes 18350080 | tf_op jit(solution)/shard_map/dot_general | solution.py:157
  553.3 1.2 copy-done.11
  554.8 2.1 collective-permute-start.1
  557.0 109.0 %gather_fusion.1 = f32[32768,32]{1,0:T(8,128)} fusion(f32[32,128]{0,1:T(8,128)S(1)} %copy.120, s32[32768]{0:T(1024)S(1)} %fusion.84), kind=kCustom, calls=%fused_computation.1 | custom fusion | bytes 8519680 | tf_op jit(solution)/shard_map/gather | solution.py:174
  666.1 11.7 %copy.121 = f32[256,128,32]{1,0,2:T(8,128)} copy(f32[256,128,32]{2,1,0:T(8,128)} %bitcast.234) | data formatting | bytes 8388608 | tf_op jit(solution)/shard_map/gather | solution.py:174
  677.8 1.7 copy.117
  679.5 0.9 maximum_convert_fusion.1
  680.4 2.8 fusion.5
  683.4 2.6 collective-permute-start.2
  686.1 6.2 collective-permute-done.2
  694.5 1.5 copy-done.2
  697.4 2.4 fusion.37
  699.9 1.0 copy.124
  (105 shorter events, 14.8 us)
Async XLA Ops:
  6.5 302.7 %copy-start = (bf16[512,512]{1,0:T(8,128)(2,1)S(1)}, bf16[512,512]{1,0:T(8,128)(2,1)}, u32[]{:S(2)}) copy-start(bf16[512,512]{1,0:T(8,128)(2,1)} %param.16) | copy-start | bytes 1572868
  15.4 9.4 %copy-start.12 = (bf16[512,3,512]{2,0,1:T(8,128)(2,1)S(1)}, bf16[512,3,512]{2,0,1:T(8,128)(2,1)}, u32[]{:S(2)}) copy-start(bf16[512,3,512]{2,0,1:T(8,128)(2,1)} %param.17) | copy-start | bytes 4718596
  15.4 417.6 %all-to-all-start = ((bf16[32,128,3,512]{1,3,2,0:T(8,128)(2,1)}), bf16[32,128,3,512]{1,3,2,0:T(8,128)(2,1)}, u32[]{:S(2)}, u32[]{:S(2)}) async-start(bf16[32,128,3,512]{1,3,2,0:T(8,128)(2,1)} %stack.17), calls=%async_computation | async-start | bytes 25165824 | tf_op jit(solution)/shard_map/all_to_all | solution.py:155
  24.8 1.7 copy-start.19
  24.8 287.5 %all-gather.4.cloned.1.call-start = ((), (), s32[]{:S(2)}) async-start(), calls=%async_computation.1 | async-start | bytes 1081344 | tf_op jit(solution)/shard_map/all_gather | solution.py:18
  26.4 6.0 copy-start.16
  26.4 6.0 copy-start.17
  26.4 7.0 copy-start.18
  26.4 7.3 %copy-start.13 = (f32[3,3,512]{2,1,0:T(4,128)S(1)}, f32[3,3,512]{2,1,0:T(4,128)}, u32[]{:S(2)}) copy-start(f32[3,3,512]{2,1,0:T(4,128)} %param.18) | copy-start | bytes 55300
  28.9 1.2 copy-start.10
  30.4 210.5 %collective-permute-start = (bf16[2,3,512]{0,2,1:T(8,128)(2,1)S(1)}, bf16[2,3,512]{0,2,1:T(8,128)(2,1)S(1)}, u32[]{:S(2)}, u32[]{:S(2)}) collective-permute-start(bf16[2,3,512]{0,2,1:T(8,128)(2,1)S(1)} %bitcast.250), channel_id=1, source_target_pairs={{0,8},{8,16},{16,24},{24,32},{32,40},{40,48},{48,56},{56,64},{64,7... | collective-permute-start | bytes 18440 | tf_op jit(solution)/shard_map/ppermute | solution.py:13
  33.4 337.0 %all-gather.6.cloned.1.call-start = ((), (), s32[]{:S(2)}) async-start(), calls=%async_computation.2 | async-start | bytes 1081344 | tf_op jit(solution)/shard_map/all_gather | solution.py:18
  244.6 1.8 copy-start.4
  244.7 0.9 copy-start.8
  246.4 1.0 copy-start.5
  248.1 293.7 %all-gather.8.cloned.1.call-start = ((), (), s32[]{:S(2)}) async-start(), calls=%async_computation.3 | async-start | bytes 4718592 | tf_op jit(solution)/shard_map/all_gather | solution.py:153
  303.6 5.5 copy-start.22
  395.7 2.4 copy-start.7
  398.2 1.2 copy-start.6
  398.2 1.3 copy-start.9
  398.2 1.3 copy-start.20
  541.8 15.1 %copy-start.14 = (f32[3,3,512]{2,1,0:T(4,128)S(1)}, f32[3,3,512]{2,1,0:T(4,128)}, u32[]{:S(2)}) copy-start(f32[3,3,512]{2,1,0:T(4,128)} %param.24) | copy-start | bytes 55300
  541.8 15.2 %copy-start.15 = (f32[32,128]{1,0:T(8,128)S(1)}, f32[32,128]{1,0:T(8,128)}, u32[]{:S(2)}) copy-start(f32[32,128]{1,0:T(8,128)} %param.25) | copy-start | bytes 49156
  553.3 1.2 copy-start.11
  554.8 124.8 %collective-permute-start.1 = (bf16[2,3,512]{0,2,1:T(8,128)(2,1)S(1)}, bf16[2,3,512]{0,2,1:T(8,128)(2,1)S(1)}, u32[]{:S(2)}, u32[]{:S(2)}) collective-permute-start(bf16[2,3,512]{0,2,1:T(8,128)(2,1)S(1)} %bitcast.251), channel_id=1, source_target_pairs={{0,8},{8,16},{16,24},{24,32},{32,40},{40,48},{48,56},{56,64},{64,7... | collective-permute-start | bytes 18440 | tf_op jit(solution)/shard_map/ppermute | solution.py:13
  683.2 9.9 %copy-start.3 = (f32[512,3,512]{0,2,1:T(8,128)}, f32[512,3,512]{0,2,1:T(8,128)S(1)}, u32[]{:S(2)}) copy-start(f32[512,3,512]{0,2,1:T(8,128)S(1)} %fusion.5) | copy-start | bytes 9437188
  683.4 9.0 %collective-permute-start.2 = (bf16[128,512]{0,1:T(8,128)(2,1)S(1)}, bf16[128,512]{0,1:T(8,128)(2,1)S(1)}, u32[]{:S(2)}, u32[]{:S(2)}) collective-permute-start(bf16[128,512]{0,1:T(8,128)(2,1)S(1)} %slice_bitcast_fusion.6), channel_id=1, source_target_pairs={{0,8},{8,16},{16,24},{24,32},{32,40},{40,48},{48,56},{56,64},{64,7... | collective-permute-start | bytes 393224 | tf_op jit(solution)/shard_map/ppermute | solution.py:13
  693.8 2.2 copy-start.2
  696.5 0.9 copy-start.21
  696.5 4.4 copy-start.1
Sparse Core Ops, SparseCore 0:
  33.5 112.5 all-gather.3
  248.2 122.1 all-gather.5
  433.0 108.7 all-gather.7
